TPU v7x, 256 devices: a whole 4x4x8 slice. The times are simulated.
256 devices in a mesh: dp: 32 (over y, z), tensor: 8 (over x, core).
Axes of the slice: x: 4, y: 4, z: 8, core: 2. Of those that a mesh axis runs over, the one named last changes fastest.
Arguments:
- queries: bfloat16 [256, 6, 8192], P('dp', None, 'tensor'), may hold values from -150 to 150
- new_keys: bfloat16 [256, 6, 1024], P('dp', None, 'tensor'), may hold values from -6 to 6
- new_values: bfloat16 [256, 6, 1024], P('dp', None, 'tensor'), may hold values from -6 to 6
- key_cache: bfloat16 [256, 256, 1024], P('dp', None, 'tensor'), may hold values from -6 to 6
- value_cache: bfloat16 [256, 256, 1024], P('dp', None, 'tensor'), may hold values from -6 to 6
- cache_lengths: int32 [256], P('dp'), may hold values from 32 to 256, as said below
- accepted: int32 [256], P('tensor'), may hold values from 1 to 6
- residual: bfloat16 [256, 6, 8192], P('tensor', None, 'dp'), may hold values from -6 to 6
- out_weight: bfloat16 [8192, 8192], P('tensor', 'dp'), may hold values from -0.0625 to 0.0625
- draft_weight: bfloat16 [8192, 8192], P('tensor', 'dp'), may hold values from -0.0625 to 0.0625
Outputs:
- verified: bfloat16 [256, 6, 8192], P('tensor', None, 'dp')
- drafted: bfloat16 [5, 256, 8192], P(None, 'tensor', 'dp')
Inputs may be any that keep to these rules, and one draw needn't show every extreme that they name: `cache_lengths`: every draw has a window with all 256 slots live.
All inputs are finite; a program needn't handle non-finite values.
Results may differ from a plain program's by a relative error of at most 0.008.
Values may be sent and summed in bfloat16 or wider, within the bound.
No kernel may reach another device: no remote copies, remote signals or barrier semaphores. Data moves between devices by JAX's collectives and lax.ppermute only.
A program may use at most 64 MiB of HBM per device.

v0:
```python
import jax
import jax.numpy as jnp
from jax import lax
from jax.sharding import PartitionSpec as P

HD = 128
STEPS = 5


def spread(block, axis):
    copies = jnp.broadcast_to(block[None], (lax.axis_size(axis),) + block.shape)
    return lax.all_to_all(copies, axis, split_axis=0, concat_axis=0, tiled=True)


def accepted_of_my_windows(accepted):
    dp_size, tensor_size = (lax.axis_size("dp"), lax.axis_size("tensor"))
    ratio = dp_size // tensor_size
    pairs = []
    for j in range(dp_size):
        for i in range(tensor_size):
            source = (ratio * i + j % ratio) * tensor_size + j // ratio
            pairs.append((source, j * tensor_size + i))
    block = lax.ppermute(accepted, ("dp", "tensor"), pairs)
    rows = accepted.shape[0] // ratio
    return lax.dynamic_slice_in_dim(block, lax.axis_index("dp") % ratio * rows, rows, 0)


def pick(rows, accepted):
    chosen = jnp.arange(rows.shape[1])[None, :] == (accepted - 1)[:, None]
    return jnp.sum(
        jnp.where(chosen[:, :, None], rows, jnp.zeros((), rows.dtype)), axis=1, dtype=rows.dtype
    )


def per_device(
    queries,
    new_keys,
    new_values,
    key_cache,
    value_cache,
    cache_lengths,
    accepted,
    residual,
    out_weight,
    draft_weight,
):
    windows_here, tokens_here, query_width = queries.shape
    cache_size = key_cache.shape[1]
    kv_here = new_keys.shape[2] // HD
    group_size = query_width // HD // kv_here
    tensor_size = lax.axis_size("tensor")
    own_accepted = accepted_of_my_windows(accepted)
    draft_columns = lax.all_gather(draft_weight, "tensor", axis=0, tiled=True)
    query_split = queries.reshape(windows_here, tokens_here, kv_here, group_size, HD)
    keys_cached = key_cache.reshape(windows_here, cache_size, kv_here, HD)
    keys_fresh = new_keys.reshape(windows_here, tokens_here, kv_here, HD)
    score_cache = jnp.einsum(
        "wtkgd,wpkd->wkgtp", query_split, keys_cached, preferred_element_type=jnp.float32
    ) * HD ** (-0.5)
    score_fresh = jnp.einsum(
        "wtkgd,wpkd->wkgtp", query_split, keys_fresh, preferred_element_type=jnp.float32
    ) * HD ** (-0.5)
    live_cache = (jnp.arange(cache_size)[None, :] < cache_lengths[:, None])[:, None, None, None, :]
    live_fresh = jnp.arange(tokens_here)[None, :] <= jnp.arange(tokens_here)[:, None]
    scores = jnp.concatenate(
        [
            jnp.where(live_cache, score_cache, -jnp.inf),
            jnp.where(live_fresh, score_fresh, -jnp.inf),
        ],
        axis=-1,
    )
    largest = jnp.max(scores, axis=-1, keepdims=True)
    powered = jnp.exp(scores - largest)
    weights = (powered / jnp.sum(powered, axis=-1, keepdims=True)).astype(jnp.bfloat16)
    values_cached = value_cache.reshape(windows_here, cache_size, kv_here, HD)
    values_fresh = new_values.reshape(windows_here, tokens_here, kv_here, HD)
    mixed_rows = jnp.einsum(
        "wkgtp,wpkd->wtkgd",
        weights[..., :cache_size],
        values_cached,
        preferred_element_type=jnp.float32,
    )
    mixed_rows = mixed_rows + jnp.einsum(
        "wkgtp,wpkd->wtkgd",
        weights[..., cache_size:],
        values_fresh,
        preferred_element_type=jnp.float32,
    )
    attended = mixed_rows.astype(jnp.bfloat16).reshape(windows_here, tokens_here, query_width)
    picked_rows = spread(pick(attended, own_accepted), "dp").reshape(-1, query_width)
    picked_part = jnp.dot(picked_rows, out_weight, preferred_element_type=jnp.float32)
    block_windows, block_tokens, block_cols = residual.shape
    shares = lax.all_to_all(
        picked_part.astype(jnp.bfloat16).reshape(tensor_size, block_windows, block_cols),
        "tensor",
        split_axis=0,
        concat_axis=0,
        tiled=True,
    )
    current = (
        pick(residual, accepted).astype(jnp.float32) + jnp.sum(shares.astype(jnp.float32), axis=0)
    ).astype(jnp.bfloat16)
    partial_out = jnp.dot(
        lax.all_gather(
            attended.reshape(windows_here * tokens_here, query_width), "dp", axis=0, tiled=True
        ),
        out_weight,
        preferred_element_type=jnp.float32,
    )
    summed = lax.psum_scatter(partial_out, "tensor", scatter_dimension=0, tiled=True)
    flat_residual = residual.reshape(block_windows * block_tokens, block_cols).astype(jnp.float32)
    verified = (
        (flat_residual + summed)
        .astype(jnp.bfloat16)
        .reshape(block_windows, block_tokens, block_cols)
    )
    columns = draft_columns.reshape(-1, block_cols, draft_columns.shape[1])
    results = []
    for draft_step in range(STEPS):
        inputs = spread(current, "dp")
        product = jnp.einsum("jwk,jkn->wn", inputs, columns, preferred_element_type=jnp.float32)
        current = jnp.tanh(2.0 * product).astype(jnp.bfloat16)
        results.append(current)
    return (verified, jnp.stack(results))


def solution(mesh):
    placed = (
        P("dp", None, "tensor"),
        P("dp", None, "tensor"),
        P("dp", None, "tensor"),
        P("dp", None, "tensor"),
        P("dp", None, "tensor"),
        P("dp"),
        P("tensor"),
        P("tensor", None, "dp"),
        P("tensor", "dp"),
        P("tensor", "dp"),
    )
    return jax.shard_map(
        per_device,
        mesh=mesh,
        in_specs=placed,
        out_specs=(P("tensor", None, "dp"), P(None, "tensor", "dp")),
        check_vma=False,
    )
```

profile of v0, /device:TPU:32, one launch (start us, length us, event | category | flops | bytes accessed | tf_op | source)
XLA Modules:
  0.0 202.9 jit_solution(7244637274583813440)
XLA Ops:
  8.0 1.3 collective-permute-start
  10.0 1.2 fusion.35
  11.2 1.4 fusion.34
  14.1 1.3 fusion.29
  16.1 0.9 broadcast_in_dim.104
  16.9 19.1 %all-to-all-start = ((bf16[32,8,1024]{2,1,0:T(8,128)(2,1)}), bf16[32,8,1024]{2,1,0:T(8,128)(2,1)S(1)}, u32[]{:S(2)}, u32[]{:S(2)}) async-start(bf16[32,8,1024]{2,1,0:T(8,128)(2,1)} %broadcast_in_dim.104), calls=%async_computation.1 | async-start | bytes 1048576 | tf_op jit(solution)/shard_map/all_to_all | solution.py:12
  36.1 15.0 %all-to-all-done = bf16[32,8,1024]{2,1,0:T(8,128)(2,1)S(1)} async-done(((bf16[32,8,1024]{2,1,0:T(8,128)(2,1)}), bf16[32,8,1024]{2,1,0:T(8,128)(2,1)S(1)}, u32[]{:S(2)}, u32[]{:S(2)}) %all-to-all-start) | async-done | bytes 524320 | tf_op jit(solution)/shard_map/all_to_all | solution.py:12
  51.1 1.0 convolution_convert_fusion
  52.0 3.4 %all-to-all-start.1 = ((bf16[8,32,256]{2,1,0:T(8,128)(2,1)}), bf16[8,32,256]{2,1,0:T(8,128)(2,1)S(1)}, u32[]{:S(2)}, u32[]{:S(2)}) async-start(bf16[8,32,256]{2,1,0:T(8,128)(2,1)} %bitcast.19), calls=%async_computation.2 | async-start | bytes 262144 | tf_op jit(solution)/shard_map/all_to_all | solution.py:93
  55.5 5.9 %all-to-all-done.1 = bf16[8,32,256]{2,1,0:T(8,128)(2,1)S(1)} async-done(((bf16[8,32,256]{2,1,0:T(8,128)(2,1)}), bf16[8,32,256]{2,1,0:T(8,128)(2,1)S(1)}, u32[]{:S(2)}, u32[]{:S(2)}) %all-to-all-start.1) | async-done | bytes 131104 | tf_op jit(solution)/shard_map/all_to_all | solution.py:93
  61.6 23.8 %all_to_all.35 = bf16[32,32,256]{2,1,0:T(8,128)(2,1)S(1)} all-to-all(bf16[32,32,256]{2,1,0:T(8,128)(2,1)S(1)} %broadcast_in_dim.105), channel_id=1, replica_groups=mesh['dp'=32,'tensor'=8] {'dp'}, dimensions={0} | all-to-all | bytes 1048576 | tf_op jit(solution)/shard_map/all_to_all | solution.py:12
  85.4 3.2 %bitcast_dynamic-update-slice_fusion.3 = (bf16[5,32,256]{2,1,0:T(8,128)(2,1)S(1)}, bf16[32,256]{1,0:T(8,128)(2,1)S(1)}) fusion(bf16[32,32,256]{2,1,0:T(8,128)(2,1)S(1)} %all_to_all.35, bf16[32,256,256]{2,1,0:T(8,128)(2,1)} %bitcast.131), kind=kOutput, calls=%fused_computation.55 | convolution fusion | flops 134234112 | bytes 4751360 | tf_op jit(solution)/shard_map/jwk,jkn->wn/dot_general | solution.py:121
  88.6 23.2 %all_to_all.36 = bf16[32,32,256]{2,1,0:T(8,128)(2,1)S(1)} all-to-all(bf16[32,32,256]{2,1,0:T(8,128)(2,1)S(1)} %broadcast_in_dim.106), channel_id=1, replica_groups=mesh['dp'=32,'tensor'=8] {'dp'}, dimensions={0} | all-to-all | bytes 1048576 | tf_op jit(solution)/shard_map/all_to_all | solution.py:12
  112.7 0.9 broadcast_in_dim.107
  113.6 5.5 %all-to-all-start.4 = ((bf16[32,32,256]{2,1,0:T(8,128)(2,1)}), bf16[32,32,256]{2,1,0:T(8,128)(2,1)S(1)}, u32[]{:S(2)}, u32[]{:S(2)}) async-start(bf16[32,32,256]{2,1,0:T(8,128)(2,1)} %broadcast_in_dim.107), calls=%async_computation.5 | async-start | bytes 1048576 | tf_op jit(solution)/shard_map/all_to_all | solution.py:12
  119.2 18.9 %all-gather.3.cloned.1.call-done = bf16[1536,1024]{1,0:T(8,128)(2,1)} async-done(((bf16[48,1024]{1,0:T(8,128)(2,1)}), bf16[1536,1024]{1,0:T(8,128)(2,1)}) %all-gather.3.cloned.1.call-update) | async-done | bytes 3145744 | tf_op jit(solution)/shard_map/all_gather | solution.py:104
  138.1 4.1 %fusion.36 = f32[1536,256]{1,0:T(8,128)} fusion(bf16[1536,1024]{1,0:T(8,128)(2,1)} %all-gather.3.cloned.1.call-done, bf16[1024,256]{1,0:T(8,128)(2,1)S(1)} %copy-done), kind=kOutput, calls=%fused_computation.66 | convolution fusion | flops 805306368 | bytes 5242880 | tf_op jit(solution)/shard_map/dot_general | solution.py:103
  142.2 3.2 %bitcast_dynamic-update-slice_fusion.1 = (bf16[5,32,256]{2,1,0:T(8,128)(2,1)S(1)}, bf16[32,256]{1,0:T(8,128)(2,1)S(1)}) fusion(bf16[5,32,256]{2,1,0:T(8,128)(2,1)S(1)} %get-tuple-element.14, bf16[32,32,256]{2,1,0:T(8,128)(2,1)S(1)} %all-to-all-done.4, bf16[32,256,256]{2,1,0:T(8,128)(2,1)} %bitcast.132), kind=kOutput, calls=%fused_computation.53 | convolution fusion | flops 134234112 | bytes 4751360 | tf_op jit(solution)/shard_map/jwk,jkn->wn/dot_general | solution.py:121
  145.5 24.1 %all_to_all.37 = bf16[32,32,256]{2,1,0:T(8,128)(2,1)S(1)} all-to-all(bf16[32,32,256]{2,1,0:T(8,128)(2,1)S(1)} %broadcast_in_dim.108), channel_id=1, replica_groups=mesh['dp'=32,'tensor'=8] {'dp'}, dimensions={0} | all-to-all | bytes 1048576 | tf_op jit(solution)/shard_map/all_to_all | solution.py:12
  170.4 0.9 broadcast_in_dim.109
  171.3 4.8 %all-to-all-start.6 = ((bf16[32,32,256]{2,1,0:T(8,128)(2,1)}), bf16[32,32,256]{2,1,0:T(8,128)(2,1)S(1)}, u32[]{:S(2)}, u32[]{:S(2)}) async-start(bf16[32,32,256]{2,1,0:T(8,128)(2,1)} %broadcast_in_dim.109), calls=%async_computation.7 | async-start | bytes 1048576 | tf_op jit(solution)/shard_map/all_to_all | solution.py:12
  176.5 0.9 add_convert_fusion
  178.1 14.5 %all-to-all-done.6 = bf16[32,32,256]{2,1,0:T(8,128)(2,1)S(1)} async-done(((bf16[32,32,256]{2,1,0:T(8,128)(2,1)}), bf16[32,32,256]{2,1,0:T(8,128)(2,1)S(1)}, u32[]{:S(2)}, u32[]{:S(2)}) %all-to-all-start.6) | async-done | bytes 524320 | tf_op jit(solution)/shard_map/all_to_all | solution.py:12
  192.7 3.0 %fusion.22 = bf16[5,32,256]{2,1,0:T(8,128)(2,1)S(1)} fusion(bf16[5,32,256]{2,1,0:T(8,128)(2,1)S(1)} %get-tuple-element.18, bf16[32,32,256]{2,1,0:T(8,128)(2,1)S(1)} %all-to-all-done.6, bf16[32,256,256]{2,1,0:T(8,128)(2,1)} %bitcast.133), kind=kOutput, calls=%fused_computation.31 | convolution fusion | flops 134234112 | bytes 4734976 | tf_op jit(solution)/shard_map/jwk,jkn->wn/dot_general | solution.py:121
  (46 shorter events, 7.3 us)
Async XLA Ops:
  7.2 43.9 %copy-start = (bf16[1024,256]{1,0:T(8,128)(2,1)S(1)}, bf16[1024,256]{1,0:T(8,128)(2,1)}, u32[]{:S(2)}) copy-start(bf16[1024,256]{1,0:T(8,128)(2,1)} %param.18) | copy-start | bytes 1572868
  7.2 28.9 %copy-start.5 = (s32[32]{0:T(128)S(1)}, s32[32]{0:T(128)}, u32[]{:S(2)}) copy-start(s32[32]{0:T(128)} %param.16) | copy-start | bytes 388
  7.2 48.2 %copy-start.3 = (bf16[32,6,256]{2,0,1:T(8,128)(2,1)S(1)}, bf16[32,6,256]{2,0,1:T(8,128)(2,1)}, u32[]{:S(2)}) copy-start(bf16[32,6,256]{2,0,1:T(8,128)(2,1)} %param.17) | copy-start | bytes 294916
  7.2 78.2 %all-gather.5.cloned.1.call-start = ((), (), s32[]{:S(2)}) async-start(), calls=%async_computation.10 | async-start | bytes 4718592 | tf_op jit(solution)/shard_map/all_gather | solution.py:53
  7.9 130.1 %all-gather.3.cloned.1.call-start = ((), (), s32[]{:S(2)}) async-start(), calls=%async_computation.8 | async-start | bytes 3244032 | tf_op jit(solution)/shard_map/all_gather | solution.py:104
  8.0 6.0 %collective-permute-start = (s32[32]{0:T(128)}, s32[32]{0:T(128)S(1)}, u32[]{:S(2)}, u32[]{:S(2)}) collective-permute-start(s32[32]{0:T(128)} %param.16), channel_id=1, source_target_pairs={{0,0},{32,1},{64,2},{96,3},{128,4},{160,5},{192,6},{224,7},{8,8},{... | collective-permute-start | bytes 392 | tf_op jit(solution)/shard_map/ppermute | solution.py:23
  16.9 34.2 %all-to-all-start = ((bf16[32,8,1024]{2,1,0:T(8,128)(2,1)}), bf16[32,8,1024]{2,1,0:T(8,128)(2,1)S(1)}, u32[]{:S(2)}, u32[]{:S(2)}) async-start(bf16[32,8,1024]{2,1,0:T(8,128)(2,1)} %broadcast_in_dim.104), calls=%async_computation.1 | async-start | bytes 1048576 | tf_op jit(solution)/shard_map/all_to_all | solution.py:12
  52.0 9.4 %all-to-all-start.1 = ((bf16[8,32,256]{2,1,0:T(8,128)(2,1)}), bf16[8,32,256]{2,1,0:T(8,128)(2,1)S(1)}, u32[]{:S(2)}, u32[]{:S(2)}) async-start(bf16[8,32,256]{2,1,0:T(8,128)(2,1)} %bitcast.19), calls=%async_computation.2 | async-start | bytes 262144 | tf_op jit(solution)/shard_map/all_to_all | solution.py:93
  85.4 26.5 %copy-start.1 = (bf16[8192,256]{1,0:T(8,128)(2,1)S(1)}, bf16[8192,256]{1,0:T(8,128)(2,1)}, u32[]{:S(2)}) copy-start(bf16[8192,256]{1,0:T(8,128)(2,1)} %all-gather.5.cloned.1.call-done) | copy-start | bytes 12582916
  113.6 28.6 %all-to-all-start.4 = ((bf16[32,32,256]{2,1,0:T(8,128)(2,1)}), bf16[32,32,256]{2,1,0:T(8,128)(2,1)S(1)}, u32[]{:S(2)}, u32[]{:S(2)}) async-start(bf16[32,32,256]{2,1,0:T(8,128)(2,1)} %broadcast_in_dim.107), calls=%async_computation.5 | async-start | bytes 1048576 | tf_op jit(solution)/shard_map/all_to_all | solution.py:12
  119.1 57.4 %reduce-scatter.2.cloned.1.call-start = ((), (), s32[]{:S(2)}) async-start(), calls=%async_computation.9 | async-start | bytes 1769472 | tf_op jit(solution)/shard_map/reduce_scatter | solution.py:110
  142.2 27.4 %copy-start.2 = (bf16[8192,256]{1,0:T(8,128)(2,1)S(1)}, bf16[8192,256]{1,0:T(8,128)(2,1)}, u32[]{:S(2)}) copy-start(bf16[8192,256]{1,0:T(8,128)(2,1)} %all-gather.5.cloned.1.call-done) | copy-start | bytes 12582916
  171.3 21.4 %all-to-all-start.6 = ((bf16[32,32,256]{2,1,0:T(8,128)(2,1)}), bf16[32,32,256]{2,1,0:T(8,128)(2,1)S(1)}, u32[]{:S(2)}, u32[]{:S(2)}) async-start(bf16[32,32,256]{2,1,0:T(8,128)(2,1)} %broadcast_in_dim.109), calls=%async_computation.7 | async-start | bytes 1048576 | tf_op jit(solution)/shard_map/all_to_all | solution.py:12
  195.7 0.6 copy-start.4
Sparse Core Ops, SparseCore 0:
  9.9 37.2 all-gather.4
  50.4 87.6 all-gather.2
  142.3 34.1 reduce-scatter.1
where the time goes:
time: 204 us; the launch traced here: 203 us
  blocking collectives  71.2 us (35%)
  waiting for transfers between devices  55.3 us (27%)
  starting transfers between devices  34.3 us (17%)
  matrix products  20.8 us (10%)
  between operations  14 us (7%)
  local copies, waits for them, and re-layouts  4.89 us (2%)
  other arithmetic  2.43 us (1%)
    all_to_all x3, blocking collectives, spread(): return lax.all_to_all(copies, axis, split_axis=0, concat_axis=0, tiled=True)  71.2 us
    all_to_all x3, waiting for transfers between devices, spread(): return lax.all_to_all(copies, axis, split_axis=0, concat_axis=0, tiled=True)  29.5 us
    all_to_all x3, starting transfers between devices, spread(): return lax.all_to_all(copies, axis, split_axis=0, concat_axis=0, tiled=True)  29.5 us
    all_gather x1, waiting for transfers between devices, per_device(): lax.all_gather(attended.reshape(windows_here * tokens_here, query_width),...  18.9 us
    dot_general x5, matrix products, per_device(): jnp.einsum('jwk,jkn->wn', inputs, columns, preferred_element_type=jnp.flo...  11 us
    all_to_all x1, waiting for transfers between devices, per_device(): lax.all_to_all(picked_part.astype(jnp.bfloat16).reshape(tensor_size, bloc...  5.94 us
    dot_general x1, matrix products, per_device(): jnp.dot(lax.all_gather(attended.reshape(windows_here * tokens_here, query...  4.12 us
  transfers between devices with their start and end apart: 8, of which 5 were waited for; matrix products, arithmetic and copies ran while one was open for 12% of the time, Pallas kernels for 0%

commit v1 on v0

--- a/solution.py
+++ b/solution.py
@@ -5,6 +5,11 @@
 
 HD = 128
 STEPS = 5
+
+
+def gather_from_all(x, axis, dim):
+    copies = jnp.concatenate([x] * lax.axis_size(axis), axis=dim)
+    return lax.all_to_all(copies, axis, dim, dim, tiled=True)
 
 
 def spread(block, axis):
@@ -101,9 +106,7 @@
         pick(residual, accepted).astype(jnp.float32) + jnp.sum(shares.astype(jnp.float32), axis=0)
     ).astype(jnp.bfloat16)
     partial_out = jnp.dot(
-        lax.all_gather(
-            attended.reshape(windows_here * tokens_here, query_width), "dp", axis=0, tiled=True
-        ),
+        gather_from_all(attended.reshape(windows_here * tokens_here, query_width), "dp", 0),
         out_weight,
         preferred_element_type=jnp.float32,
     )

time: 204 us -> 273 us (1.34)
  waiting for transfers between devices: 55.3 us -> 130 us
  blocking collectives: 71.2 us -> 21.5 us
  local copies, waits for them, and re-layouts: 4.89 us -> 26.5 us
  starting transfers between devices: 34.3 us -> 54.8 us
    all_to_all x0 -> x1, waiting for transfers between devices: none -> 67.2 us  [gather_from_all(): return lax.all_to_all(copies, axis, dim, dim, tiled=True)]
    all_to_all x3 -> x1, blocking collectives: 71.2 us -> 21.5 us  [spread(): return lax.all_to_all(copies, axis, split_axis=0, concat_axis=0, tiled=True)]
    all_to_all x3 -> x5, waiting for transfers between devices: 29.5 us -> 57.6 us  [spread(): return lax.all_to_all(copies, axis, split_axis=0, concat_axis=0, tiled=True)]
    unnamed x15 -> x45, local copies, waits for them, and re-layouts: 1.98 us -> 21.4 us
    all_gather x1 -> x0, waiting for transfers between devices: 18.9 us -> none  [per_device(): lax.all_gather(attended.reshape(windows_here * tokens_here, query_width),...]
    all_to_all x3 -> x5, starting transfers between devices: 29.5 us -> 45 us  [spread(): return lax.all_to_all(copies, axis, split_axis=0, concat_axis=0, tiled=True)]
    all_to_all x0 -> x1, starting transfers between devices: none -> 4.91 us  [gather_from_all(): return lax.all_to_all(copies, axis, dim, dim, tiled=True)]
  transfers between devices with their start and end apart: 8 -> 10, of which waited for: 5 -> 7; matrix products, arithmetic and copies ran while one was open for 12% -> 16% of each run, Pallas kernels for 0% -> 0%
where the time goes in v1:
time: 273 us; the launch traced here: 272 us
  waiting for transfers between devices  130 us (48%)
  starting transfers between devices  54.8 us (20%)
  local copies, waits for them, and re-layouts  26.5 us (10%)
  blocking collectives  21.5 us (8%)
  matrix products  21.1 us (8%)
  between operations  14.4 us (5%)
  other arithmetic  3.09 us (1%)
    all_to_all x1, waiting for transfers between devices, gather_from_all(): return lax.all_to_all(copies, axis, dim, dim, tiled=True)  67.2 us
    all_to_all x5, waiting for transfers between devices, spread(): return lax.all_to_all(copies, axis, split_axis=0, concat_axis=0, tiled=True)  57.6 us
    all_to_all x5, starting transfers between devices, spread(): return lax.all_to_all(copies, axis, split_axis=0, concat_axis=0, tiled=True)  45 us
    all_to_all x1, blocking collectives, spread(): return lax.all_to_all(copies, axis, split_axis=0, concat_axis=0, tiled=True)  21.5 us
    unnamed x45, local copies, waits for them, and re-layouts  21.4 us
    dot_general x5, matrix products, per_device(): jnp.einsum('jwk,jkn->wn', inputs, columns, preferred_element_type=jnp.flo...  13.1 us
  transfers between devices with their start and end apart: 10, of which 7 were waited for; matrix products, arithmetic and copies ran while one was open for 16% of the time, Pallas kernels for 0%

profile of v1, /device:TPU:32, one launch (start us, length us, event | category | flops | bytes accessed | tf_op | source)
XLA Modules:
  0.0 271.6 jit_solution(5033261812633513819)
XLA Ops:
  7.3 1.4 collective-permute-start
  10.1 1.4 fusion.34
  11.6 1.2 fusion.35
  14.8 18.9 %all-to-all-start.1 = ((bf16[32,8,1024]{2,1,0:T(8,128)(2,1)}), bf16[32,8,1024]{2,1,0:T(8,128)(2,1)S(1)}, u32[]{:S(2)}, u32[]{:S(2)}) async-start(bf16[32,8,1024]{2,1,0:T(8,128)(2,1)} %broadcast_in_dim.104), calls=%async_computation.2 | async-start | bytes 1048576 | tf_op jit(solution)/shard_map/all_to_all | solution.py:17
  47.3 1.5 all-to-all-done.1
  49.8 3.4 %all-to-all-start.2 = ((bf16[8,32,256]{2,1,0:T(8,128)(2,1)}), bf16[8,32,256]{2,1,0:T(8,128)(2,1)S(1)}, u32[]{:S(2)}, u32[]{:S(2)}) async-start(bf16[8,32,256]{2,1,0:T(8,128)(2,1)} %bitcast.21), calls=%async_computation.3 | async-start | bytes 262144 | tf_op jit(solution)/shard_map/all_to_all | solution.py:98
  53.8 5.4 %all-to-all-done.2 = bf16[8,32,256]{2,1,0:T(8,128)(2,1)S(1)} async-done(((bf16[8,32,256]{2,1,0:T(8,128)(2,1)}), bf16[8,32,256]{2,1,0:T(8,128)(2,1)S(1)}, u32[]{:S(2)}, u32[]{:S(2)}) %all-to-all-start.2) | async-done | bytes 131104 | tf_op jit(solution)/shard_map/all_to_all | solution.py:98
  60.1 8.3 %all-to-all-start.3 = ((bf16[32,32,256]{2,1,0:T(8,128)(2,1)}), bf16[32,32,256]{2,1,0:T(8,128)(2,1)S(1)}, u32[]{:S(2)}, u32[]{:S(2)}) async-start(bf16[32,32,256]{2,1,0:T(8,128)(2,1)} %broadcast_in_dim.105), calls=%async_computation.4 | async-start | bytes 1048576 | tf_op jit(solution)/shard_map/all_to_all | solution.py:17
  71.6 14.2 %all-to-all-done.3 = bf16[32,32,256]{2,1,0:T(8,128)(2,1)S(1)} async-done(((bf16[32,32,256]{2,1,0:T(8,128)(2,1)}), bf16[32,32,256]{2,1,0:T(8,128)(2,1)S(1)}, u32[]{:S(2)}, u32[]{:S(2)}) %all-to-all-start.3) | async-done | bytes 524320 | tf_op jit(solution)/shard_map/all_to_all | solution.py:17
  85.8 3.0 %constant_dynamic-update-slice_fusion.3 = (bf16[5,32,256]{2,1,0:T(8,128)(2,1)S(1)}, bf16[32,256]{1,0:T(8,128)(2,1)S(1)}) fusion(bf16[32,32,256]{2,1,0:T(8,128)(2,1)S(1)} %all-to-all-done.3, bf16[32,256,256]{2,1,0:T(8,128)(2,1)} %bitcast.195), kind=kOutput, calls=%fused_computation.84 | convolution fusion | flops 134234112 | bytes 4751360 | tf_op jit(solution)/shard_map/jwk,jkn->wn/dot_general | solution.py:124
  89.7 4.8 %all-to-all-start.4 = ((bf16[32,32,256]{2,1,0:T(8,128)(2,1)}), bf16[32,32,256]{2,1,0:T(8,128)(2,1)S(1)}, u32[]{:S(2)}, u32[]{:S(2)}) async-start(bf16[32,32,256]{2,1,0:T(8,128)(2,1)} %broadcast_in_dim.106), calls=%async_computation.5 | async-start | bytes 1048576 | tf_op jit(solution)/shard_map/all_to_all | solution.py:17
  97.8 13.7 %all-to-all-done.4 = bf16[32,32,256]{2,1,0:T(8,128)(2,1)S(1)} async-done(((bf16[32,32,256]{2,1,0:T(8,128)(2,1)}), bf16[32,32,256]{2,1,0:T(8,128)(2,1)S(1)}, u32[]{:S(2)}, u32[]{:S(2)}) %all-to-all-start.4) | async-done | bytes 524320 | tf_op jit(solution)/shard_map/all_to_all | solution.py:17
  111.5 4.9 %all-to-all-start = ((bf16[32,48,1024]{2,1,0:T(8,128)(2,1)}), bf16[32,48,1024]{2,1,0:T(8,128)(2,1)}, u32[]{:S(2)}, u32[]{:S(2)}) async-start(bf16[32,48,1024]{2,1,0:T(8,128)(2,1)} %bitcast.16), calls=%async_computation | async-start | bytes 6291456 | tf_op jit(solution)/shard_map/all_to_all | solution.py:12
  116.4 3.0 %constant_dynamic-update-slice_fusion.2 = (bf16[5,32,256]{2,1,0:T(8,128)(2,1)S(1)}, bf16[32,256]{1,0:T(8,128)(2,1)S(1)}) fusion(bf16[5,32,256]{2,1,0:T(8,128)(2,1)S(1)} %get-tuple-element.12, bf16[32,32,256]{2,1,0:T(8,128)(2,1)S(1)} %all-to-all-done.4, bf16[32,256,256]{2,1,0:T(8,128)(2,1)} %bitcast.196), kind=kOutput, calls=%fused_computation.83 | convolution fusion | flops 134234112 | bytes 4751360 | tf_op jit(solution)/shard_map/jwk,jkn->wn/dot_general | solution.py:124
  119.4 67.2 %all-to-all-done = bf16[32,48,1024]{2,1,0:T(8,128)(2,1)} async-done(((bf16[32,48,1024]{2,1,0:T(8,128)(2,1)}), bf16[32,48,1024]{2,1,0:T(8,128)(2,1)}, u32[]{:S(2)}, u32[]{:S(2)}) %all-to-all-start) | async-done | bytes 3145760 | tf_op jit(solution)/shard_map/all_to_all | solution.py:12
  187.5 8.0 %all-to-all-start.5 = ((bf16[32,32,256]{2,1,0:T(8,128)(2,1)}), bf16[32,32,256]{2,1,0:T(8,128)(2,1)S(1)}, u32[]{:S(2)}, u32[]{:S(2)}) async-start(bf16[32,32,256]{2,1,0:T(8,128)(2,1)} %broadcast_in_dim.107), calls=%async_computation.6 | async-start | bytes 1048576 | tf_op jit(solution)/shard_map/all_to_all | solution.py:17
  195.6 4.1 %fusion.36 = f32[1536,256]{1,0:T(8,128)} fusion(bf16[1536,1024]{1,0:T(8,128)(2,1)} %bitcast.17, bf16[1024,256]{1,0:T(8,128)(2,1)S(1)} %copy-done), kind=kOutput, calls=%fused_computation.97 | convolution fusion | flops 805306368 | bytes 5242880 | tf_op jit(solution)/shard_map/dot_general | solution.py:108
  199.7 13.3 %all-to-all-done.5 = bf16[32,32,256]{2,1,0:T(8,128)(2,1)S(1)} async-done(((bf16[32,32,256]{2,1,0:T(8,128)(2,1)}), bf16[32,32,256]{2,1,0:T(8,128)(2,1)S(1)}, u32[]{:S(2)}, u32[]{:S(2)}) %all-to-all-start.5) | async-done | bytes 524320 | tf_op jit(solution)/shard_map/all_to_all | solution.py:17
  213.0 3.2 %constant_dynamic-update-slice_fusion.1 = (bf16[5,32,256]{2,1,0:T(8,128)(2,1)S(1)}, bf16[32,256]{1,0:T(8,128)(2,1)S(1)}) fusion(bf16[5,32,256]{2,1,0:T(8,128)(2,1)S(1)} %get-tuple-element.14, bf16[32,32,256]{2,1,0:T(8,128)(2,1)S(1)} %all-to-all-done.5, bf16[32,256,256]{2,1,0:T(8,128)(2,1)} %bitcast.197), kind=kOutput, calls=%fused_computation.82 | convolution fusion | flops 134234112 | bytes 4751360 | tf_op jit(solution)/shard_map/jwk,jkn->wn/dot_general | solution.py:124
  216.3 21.5 %all_to_all.47 = bf16[32,32,256]{2,1,0:T(8,128)(2,1)S(1)} all-to-all(bf16[32,32,256]{2,1,0:T(8,128)(2,1)S(1)} %broadcast_in_dim.108), channel_id=1, replica_groups=mesh['dp'=32,'tensor'=8] {'dp'}, dimensions={0} | all-to-all | bytes 1048576 | tf_op jit(solution)/shard_map/all_to_all | solution.py:17
  239.5 4.9 %all-to-all-start.7 = ((bf16[32,32,256]{2,1,0:T(8,128)(2,1)}), bf16[32,32,256]{2,1,0:T(8,128)(2,1)S(1)}, u32[]{:S(2)}, u32[]{:S(2)}) async-start(bf16[32,32,256]{2,1,0:T(8,128)(2,1)} %broadcast_in_dim.109), calls=%async_computation.8 | async-start | bytes 1048576 | tf_op jit(solution)/shard_map/all_to_all | solution.py:17
  244.5 0.9 add_convert_fusion
  246.1 15.0 %all-to-all-done.7 = bf16[32,32,256]{2,1,0:T(8,128)(2,1)S(1)} async-done(((bf16[32,32,256]{2,1,0:T(8,128)(2,1)}), bf16[32,32,256]{2,1,0:T(8,128)(2,1)S(1)}, u32[]{:S(2)}, u32[]{:S(2)}) %all-to-all-start.7) | async-done | bytes 524320 | tf_op jit(solution)/shard_map/all_to_all | solution.py:17
  261.1 3.0 %fusion.22 = bf16[5,32,256]{2,1,0:T(8,128)(2,1)S(1)} fusion(bf16[5,32,256]{2,1,0:T(8,128)(2,1)S(1)} %get-tuple-element.18, bf16[32,32,256]{2,1,0:T(8,128)(2,1)S(1)} %all-to-all-done.7, bf16[32,256,256]{2,1,0:T(8,128)(2,1)} %bitcast.198), kind=kOutput, calls=%fused_computation.31 | convolution fusion | flops 134234112 | bytes 4734976 | tf_op jit(solution)/shard_map/jwk,jkn->wn/dot_general | solution.py:124
  (78 shorter events, 30.9 us)
Async XLA Ops:
  7.2 41.6 %copy-start = (bf16[1024,256]{1,0:T(8,128)(2,1)S(1)}, bf16[1024,256]{1,0:T(8,128)(2,1)}, u32[]{:S(2)}) copy-start(bf16[1024,256]{1,0:T(8,128)(2,1)} %param.18) | copy-start | bytes 1572868
  7.2 6.0 %copy-start.4 = (bf16[8,6,128]{2,0,1:T(8,128)(2,1)S(1)}, bf16[8,6,128]{2,0,1:T(8,128)(2,1)}, u32[]{:S(2)}) copy-start(bf16[8,6,128]{2,0,1:T(8,128)(2,1)} %param.12) | copy-start | bytes 36868
  7.2 6.2 %copy-start.3 = (bf16[32,6,256]{2,0,1:T(8,128)(2,1)S(1)}, bf16[32,6,256]{2,0,1:T(8,128)(2,1)}, u32[]{:S(2)}) copy-start(bf16[32,6,256]{2,0,1:T(8,128)(2,1)} %param.17) | copy-start | bytes 294916
  7.2 6.5 %copy-start.2 = (bf16[8,256,128]{2,1,0:T(8,128)(2,1)S(1)}, bf16[8,256,128]{2,1,0:T(8,128)(2,1)}, u32[]{:S(2)}) copy-start(bf16[8,256,128]{2,1,0:T(8,128)(2,1)} %param.14) | copy-start | bytes 1572868
  7.2 78.6 %all-gather.2.cloned.1.call-start = ((), (), s32[]{:S(2)}) async-start(), calls=%async_computation.10 | async-start | bytes 4718592 | tf_op jit(solution)/shard_map/all_gather | solution.py:58
  7.3 6.2 %collective-permute-start = (s32[32]{0:T(128)}, s32[32]{0:T(128)S(1)}, u32[]{:S(2)}, u32[]{:S(2)}) collective-permute-start(s32[32]{0:T(128)} %param.16), channel_id=1, source_target_pairs={{0,0},{32,1},{64,2},{96,3},{128,4},{160,5},{192,6},{224,7},{8,8},{... | collective-permute-start | bytes 392 | tf_op jit(solution)/shard_map/ppermute | solution.py:28
  14.8 34.0 %all-to-all-start.1 = ((bf16[32,8,1024]{2,1,0:T(8,128)(2,1)}), bf16[32,8,1024]{2,1,0:T(8,128)(2,1)S(1)}, u32[]{:S(2)}, u32[]{:S(2)}) async-start(bf16[32,8,1024]{2,1,0:T(8,128)(2,1)} %broadcast_in_dim.104), calls=%async_computation.2 | async-start | bytes 1048576 | tf_op jit(solution)/shard_map/all_to_all | solution.py:17
  49.8 9.4 %all-to-all-start.2 = ((bf16[8,32,256]{2,1,0:T(8,128)(2,1)}), bf16[8,32,256]{2,1,0:T(8,128)(2,1)S(1)}, u32[]{:S(2)}, u32[]{:S(2)}) async-start(bf16[8,32,256]{2,1,0:T(8,128)(2,1)} %bitcast.21), calls=%async_computation.3 | async-start | bytes 262144 | tf_op jit(solution)/shard_map/all_to_all | solution.py:98
  60.1 25.8 %all-to-all-start.3 = ((bf16[32,32,256]{2,1,0:T(8,128)(2,1)}), bf16[32,32,256]{2,1,0:T(8,128)(2,1)S(1)}, u32[]{:S(2)}, u32[]{:S(2)}) async-start(bf16[32,32,256]{2,1,0:T(8,128)(2,1)} %broadcast_in_dim.105), calls=%async_computation.4 | async-start | bytes 1048576 | tf_op jit(solution)/shard_map/all_to_all | solution.py:17
  89.7 21.8 %all-to-all-start.4 = ((bf16[32,32,256]{2,1,0:T(8,128)(2,1)}), bf16[32,32,256]{2,1,0:T(8,128)(2,1)S(1)}, u32[]{:S(2)}, u32[]{:S(2)}) async-start(bf16[32,32,256]{2,1,0:T(8,128)(2,1)} %broadcast_in_dim.106), calls=%async_computation.5 | async-start | bytes 1048576 | tf_op jit(solution)/shard_map/all_to_all | solution.py:17
  111.5 75.1 %all-to-all-start = ((bf16[32,48,1024]{2,1,0:T(8,128)(2,1)}), bf16[32,48,1024]{2,1,0:T(8,128)(2,1)}, u32[]{:S(2)}, u32[]{:S(2)}) async-start(bf16[32,48,1024]{2,1,0:T(8,128)(2,1)} %bitcast.16), calls=%async_computation | async-start | bytes 6291456 | tf_op jit(solution)/shard_map/all_to_all | solution.py:12
  187.5 25.5 %all-to-all-start.5 = ((bf16[32,32,256]{2,1,0:T(8,128)(2,1)}), bf16[32,32,256]{2,1,0:T(8,128)(2,1)S(1)}, u32[]{:S(2)}, u32[]{:S(2)}) async-start(bf16[32,32,256]{2,1,0:T(8,128)(2,1)} %broadcast_in_dim.107), calls=%async_computation.6 | async-start | bytes 1048576 | tf_op jit(solution)/shard_map/all_to_all | solution.py:17
  195.5 49.0 %reduce-scatter.2.cloned.1.call-start = ((), (), s32[]{:S(2)}) async-start(), calls=%async_computation.9 | async-start | bytes 1769472 | tf_op jit(solution)/shard_map/reduce_scatter | solution.py:113
  213.0 24.8 %copy-start.1 = (bf16[8192,256]{1,0:T(8,128)(2,1)S(1)}, bf16[8192,256]{1,0:T(8,128)(2,1)}, u32[]{:S(2)}) copy-start(bf16[8192,256]{1,0:T(8,128)(2,1)} %all-gather.2.cloned.1.call-done) | copy-start | bytes 12582916
  239.5 21.6 %all-to-all-start.7 = ((bf16[32,32,256]{2,1,0:T(8,128)(2,1)}), bf16[32,32,256]{2,1,0:T(8,128)(2,1)S(1)}, u32[]{:S(2)}, u32[]{:S(2)}) async-start(bf16[32,32,256]{2,1,0:T(8,128)(2,1)} %broadcast_in_dim.109), calls=%async_computation.8 | async-start | bytes 1048576 | tf_op jit(solution)/shard_map/all_to_all | solution.py:17
  264.1 0.6 copy-start.5
Sparse Core Ops, SparseCore 0:
  9.9 39.2 all-gather.1
  199.8 34.5 reduce-scatter.1
